TPU v7x, 512 devices: a whole 4x4x16 slice. The times are simulated.
512 devices in a mesh: grp: 8 (over y, x_hi), comp: 64 (over x_lo, z, core).
Axes of the slice: x: 4 (x_hi: 2, x_lo: 2; x = x_hi * 2 + x_lo), y: 4, z: 16, core: 2. Of those that a mesh axis runs over, the one named last changes fastest.
Arguments:
- features: bfloat16 [1048576, 256], P(('grp', 'comp')), may hold values from -8 to 8
- means: float32 [1024, 256], P('comp'), may hold values from -1 to 1
- variances: float32 [1024, 256], P('comp'), may hold values from 0.5 to 2
- weight_logits: float32 [1024], replicated, may hold values from -1 to 1
Outputs:
- new_means: float32 [1024, 256], replicated
- new_variances: float32 [1024, 256], replicated
- new_log_weights: float32 [1024], replicated
- row_scores: float32 [1048576], P(('grp', 'comp'))
All inputs are finite; a program needn't handle non-finite values.
Results may differ from a plain program's by a relative error of at most 0.00085.
Values sent between devices are 32-bit elements; how exact they have to be, the bound alone decides.
A program may use at most 64 MiB of HBM per device.

v0:
```python
import math
import jax
import jax.numpy as jnp
from jax import lax
from jax.sharding import PartitionSpec as P


def update_step(moments, counts, total_rows):
    width = moments.shape[1] // 2
    denominator = (counts + 1.0)[:, None]
    fresh_means = moments[:, :width] / denominator
    fresh_variances = (moments[:, width:] + 1.0) / denominator - fresh_means * fresh_means + 0.01
    fresh_weights = jnp.log((counts + 1.0) / total_rows)
    return (fresh_means, fresh_variances, fresh_weights)


def on_device(features, means, variances, weight_logits):
    owned_count = means.shape[0]
    width = means.shape[1]
    first_owned = lax.axis_index("comp") * owned_count
    log_weights = lax.dynamic_slice_in_dim(
        jax.nn.log_softmax(weight_logits), first_owned, owned_count
    )
    inverse = 1.0 / variances
    coefficient = jnp.concatenate([-0.5 * inverse, means * inverse], axis=1)
    offsets = (
        log_weights
        - 0.5 * jnp.sum(jnp.log(variances) + means * means * inverse, axis=1)
        - 0.5 * width * math.log(2.0 * math.pi)
    )
    all_coefficient, all_offsets = (
        lax.all_gather(coefficient, "comp", axis=0, tiled=True),
        lax.all_gather(offsets, "comp", axis=0, tiled=True),
    )
    total_comps = all_coefficient.shape[0]
    local_rows = features.shape[0]
    block_size = min(512, local_rows)
    moments = jnp.zeros((total_comps, 2 * width), jnp.float32)
    counts = jnp.zeros((total_comps,), jnp.float32)
    score_pieces = []
    ones_row = jnp.ones((block_size,), jnp.bfloat16)
    for block_index in range(local_rows // block_size):
        block_rows = features[block_index * block_size : (block_index + 1) * block_size]
        values = block_rows.astype(jnp.float32)
        squared = values * values
        scores = (
            jnp.dot(
                jnp.concatenate([squared, values], axis=1),
                all_coefficient.T,
                precision=lax.Precision.HIGHEST,
            )
            + all_offsets
        )
        highest = jnp.max(scores, axis=1, keepdims=True)
        exponent = jnp.exp(scores - highest)
        totals = jnp.sum(exponent, axis=1, keepdims=True)
        responsibility = (exponent / totals).astype(jnp.bfloat16)
        score_pieces.append((highest[:, 0] + jnp.log(totals[:, 0])) / width)
        moment_inputs = jnp.concatenate([block_rows, squared.astype(jnp.bfloat16)], axis=1)
        moments = moments + jnp.dot(
            responsibility.T, moment_inputs, preferred_element_type=jnp.float32
        )
        counts = counts + jnp.dot(ones_row, responsibility, preferred_element_type=jnp.float32)
    row_scores = jnp.concatenate(score_pieces, axis=0)
    total_rows = jnp.float32(
        local_rows * lax.axis_size("grp") * lax.axis_size("comp") + total_comps
    )
    owned_moments, owned_counts = (
        lax.psum_scatter(moments, "comp", scatter_dimension=0, tiled=True),
        lax.psum_scatter(counts, "comp", scatter_dimension=0, tiled=True),
    )
    summed_moments, summed_counts = lax.psum((owned_moments, owned_counts), "grp")
    owned_means, owned_variances, owned_weights = update_step(
        summed_moments, summed_counts, total_rows
    )
    fresh_means, fresh_variances, fresh_weights = (
        lax.all_gather(owned_means, "comp", axis=0, tiled=True),
        lax.all_gather(owned_variances, "comp", axis=0, tiled=True),
        lax.all_gather(owned_weights, "comp", axis=0, tiled=True),
    )
    return (fresh_means, fresh_variances, fresh_weights, row_scores)


def solution(mesh):
    return jax.shard_map(
        on_device,
        mesh=mesh,
        in_specs=(P(("grp", "comp"), None), P("comp", None), P("comp", None), P()),
        out_specs=(P(), P(), P(), P(("grp", "comp"))),
        check_vma=False,
    )
```

profile of v0, /device:TPU:1, one launch (start us, length us, event | category | flops | bytes accessed | tf_op | source)
XLA Modules:
  0.0 667.8 jit_solution(7792017935220275641)
XLA Ops:
  7.2 0.0 all-gather.4.cloned.1.call-start
  7.2 0.9 add_reduce_fusion.4
  8.1 0.6 pad_maximum_fusion
  8.7 0.0 all-gather.4.cloned.1.call-update
  8.7 0.0 reduce-scatter.2.cloned.1.call-start
  8.8 1.3 reduce_max.46
  10.1 1.9 exponential_reduce_fusion
  12.7 1.4 fusion.64
  14.7 1.3 subtract_subtract_fusion
  16.0 0.2 add_dynamic-update-slice_fusion
  16.2 112.2 %all-reduce = f32[1024]{0:T(1024)S(1)} all-reduce(f32[1024]{0:T(1024)S(1)} %add_dynamic-update-slice_fusion), channel_id=1, replica_groups=mesh['grp'=8,'comp'=64] {'comp'}, use_global_device_ids=true, to_apply=%add | all-reduce | flops 1024 | bytes 8192
  128.4 2.3 fusion.63
  130.8 0.0 copy-done.3
  130.8 1.4 fusion.38
  132.2 5.9 all-gather.4.cloned.1.call-done
  138.0 5.5 fusion.4
  143.5 0.0 copy-done
  143.5 0.0 copy-done.4
  143.5 3.6 fusion.12
  147.1 3.7 add_reduce_fusion
  150.8 4.4 fusion.3
  155.3 1.5 fusion.1
  156.8 0.0 copy-start.1
  156.8 0.0 copy-start.8
  156.8 0.0 copy-start.11
  156.9 1.4 divide_convert_fusion.2
  158.2 0.0 copy-done.8
  158.2 0.0 copy-done.11
  158.3 0.0 copy-start.6
  158.3 0.0 copy-start.10
  158.3 0.8 fusion.24
  159.0 0.2 copy-done.6
  159.2 0.1 copy-done.10
  159.3 0.7 fusion.20
  160.0 0.2 copy-done.5
  160.2 0.1 copy-done.9
  160.3 0.7 fusion.28
  161.1 0.0 copy-done.1
  161.1 0.2 copy-done.7
  161.3 2.1 add_add_fusion
  163.4 0.0 reduce-scatter.2.cloned.1.call-update
  163.4 0.0 all-gather.6.cloned.1.call-start
  164.1 0.0 copy-start.2
  164.1 0.2 fusion.49
  164.4 0.2 fusion.47
  164.6 0.3 fusion.45
  164.9 0.5 copy-done.2
  165.3 0.2 fusion.43
  165.6 104.4 %all-reduce.2 = f32[1024]{0:T(1024)S(1)} all-reduce(f32[1024]{0:T(1024)S(1)} %add_add_fusion.1), channel_id=3, replica_groups=mesh['grp'=8,'comp'=64] {'comp'}, use_global_device_ids=true, to_apply=%region_13.14.clone | all-reduce | flops 1024 | bytes 8192
  270.0 0.1 dynamic-slice.3
  270.1 114.1 %reduce-scatter.2.cloned.1.call-done = f32[16,512]{1,0:T(8,128)} async-done(((f32[1024,512]{1,0:T(8,128)}), f32[16,512]{1,0:T(8,128)}) %reduce-scatter.2.cloned.1.call-update) | async-done | bytes 32784 | tf_op jit(solution)/shard_map/reduce_scatter | solution.py:69
  384.2 35.4 %all-reduce.3 = (f32[16,512]{1,0:T(8,128)S(1)}, f32[16]{0:T(128)S(1)}) all-reduce(f32[16,512]{1,0:T(8,128)} %reduce-scatter.2.cloned.1.call-done, f32[16]{0:T(128)S(1)} %dynamic-slice.3), channel_id=1, replica_groups=mesh['grp'=8,'comp'=64] {'grp'}, use_global_device_ids=true, to_apply=%region_12.13 | all-reduce | flops 8208 | bytes 65664 | tf_op jit(solution)/shard_map/psum | solution.py:72
  419.5 0.1 log_dynamic-update-slice_fusion
  419.6 0.7 fusion.41
  420.3 0.0 all-gather.6.cloned.1.call-update
  420.4 0.0 all-gather.8.cloned.1.call-start
  420.4 0.5 all-gather.8.cloned.1.call-update
  421.0 0.6 pad_maximum_fusion.1
  421.6 115.8 %all-reduce.1 = f32[1024]{0:T(1024)} all-reduce(f32[1024]{0:T(1024)S(1)} %get-tuple-element.41), channel_id=1, replica_groups=mesh['grp'=8,'comp'=64] {'comp'}, use_global_device_ids=true, to_apply=%add.1 | all-reduce | flops 1024 | bytes 8192
  537.4 0.8 all-gather.6.cloned.1.call-done
  538.2 119.8 %all-gather.8.cloned.1.call-done = f32[1024,256]{1,0:T(8,128)} async-done(((f32[16,256]{1,0:T(8,128)}), f32[1024,256]{1,0:T(8,128)}) %all-gather.8.cloned.1.call-update) | async-done | bytes 1048592 | tf_op jit(solution)/shard_map/all_gather | solution.py:78
  658.0 2.4 copy.12
  660.3 0.0 copy-done.12
  660.3 1.0 copy.13
  (12 shorter events, 0.0 us)
Async XLA Ops:
  7.2 130.9 %all-gather.4.cloned.1.call-start = ((), (), s32[]{:S(2)}) async-start(), calls=%async_computation.1 | async-start | bytes 2129920 | tf_op jit(solution)/shard_map/all_gather | solution.py:32
  8.7 375.5 %reduce-scatter.2.cloned.1.call-start = ((), (), s32[]{:S(2)}) async-start(), calls=%async_computation.2 | async-start | bytes 2129920 | tf_op jit(solution)/shard_map/reduce_scatter | solution.py:69
  128.4 2.3 copy-start.3
  138.0 5.5 copy-start
  138.0 5.5 copy-start.4
  156.8 4.2 copy-start.1
  156.8 1.4 copy-start.8
  156.8 1.4 copy-start.11
  158.3 1.0 copy-start.6
  158.3 1.0 copy-start.10
  159.3 0.9 copy-start.5
  159.3 1.0 copy-start.9
  160.3 0.9 copy-start.7
  163.4 374.8 %all-gather.6.cloned.1.call-start = ((), (), s32[]{:S(2)}) async-start(), calls=%async_computation.3 | async-start | bytes 1064960 | tf_op jit(solution)/shard_map/all_gather | solution.py:77
  164.1 1.2 copy-start.2
  420.4 237.6 %all-gather.8.cloned.1.call-start = ((), (), s32[]{:S(2)}) async-start(), calls=%async_computation.4 | async-start | bytes 1064960 | tf_op jit(solution)/shard_map/all_gather | solution.py:78
  658.0 2.4 copy-start.12
Sparse Core Ops, SparseCore 0:
  10.2 127.8 all-gather.3
  163.5 220.5 reduce-scatter.1
  420.5 117.6 all-gather.5
  541.0 116.9 all-gather.7
where the time goes:
time: 669 us; the launch traced here: 668 us
  blocking collectives  368 us (55%)
  waiting for transfers between devices  241 us (36%)
  matrix products  22.6 us (3%)
  between operations  15.9 us (2%)
  other arithmetic  14.3 us (2%)
    unnamed x3, blocking collectives  332 us
    all_gather x1, waiting for transfers between devices, on_device(): lax.all_gather(owned_variances, 'comp', axis=0, tiled=True)  120 us
    reduce_scatter x1, waiting for transfers between devices, on_device(): lax.psum_scatter(moments, 'comp', scatter_dimension=0, tiled=True)  114 us
    psum x1, blocking collectives, on_device(): lax.psum((owned_moments, owned_counts), 'grp')  35.4 us
    dot_general x4, matrix products, on_device(): jnp.dot(jnp.concatenate([squared, values], axis=1), all_coefficient.T, pr...  17.2 us
  transfers between devices with their start and end apart: 4, of which 4 were waited for; matrix products, arithmetic and copies ran while one was open for 2% of the time, Pallas kernels for 0%

commit v1 on v0

--- a/solution.py
+++ b/solution.py
@@ -3,6 +3,19 @@
 import jax.numpy as jnp
 from jax import lax
 from jax.sharding import PartitionSpec as P
+
+
+def ends_save(out_dim, ax_name, unit):
+    item_now = jnp.concatenate(
+        lax.all_to_all(
+            jnp.stack([unit] * lax.axis_size(ax_name)),
+            axis_name=ax_name,
+            split_axis=0,
+            concat_axis=0,
+        ),
+        axis=out_dim,
+    )
+    return item_now
 
 
 def update_step(moments, counts, total_rows):
@@ -75,7 +88,7 @@
     )
     fresh_means, fresh_variances, fresh_weights = (
         lax.all_gather(owned_means, "comp", axis=0, tiled=True),
-        lax.all_gather(owned_variances, "comp", axis=0, tiled=True),
+        ends_save(0, "comp", owned_variances),
         lax.all_gather(owned_weights, "comp", axis=0, tiled=True),
     )
     return (fresh_means, fresh_variances, fresh_weights, row_scores)

time: 669 us -> 592 us (0.88)
  waiting for transfers between devices: 241 us -> 121 us
  blocking collectives: 368 us -> 395 us
  starting transfers between devices: 0.16 us -> 15.3 us
    all_gather x1 -> x0, waiting for transfers between devices: 120 us -> none  [on_device(): lax.all_gather(owned_variances, 'comp', axis=0, tiled=True)]
    unnamed x3, blocking collectives: 332 us -> 360 us
    all_to_all x0 -> x1, starting transfers between devices: none -> 15.2 us  [ends_save(): lax.all_to_all(jnp.stack([unit] * lax.axis_size(ax_name)), axis_name=ax_n...]
  transfers between devices with their start and end apart: 4 -> 4, of which waited for: 4 -> 2; matrix products, arithmetic and copies ran while one was open for 2% -> 2% of each run, Pallas kernels for 0% -> 0%
where the time goes in v1:
time: 592 us; the launch traced here: 591 us
  blocking collectives  395 us (67%)
  waiting for transfers between devices  121 us (20%)
  matrix products  22.6 us (4%)
  between operations  15.9 us (3%)
  starting transfers between devices  15.3 us (3%)
  other arithmetic  14.3 us (2%)
  local copies, waits for them, and re-layouts  6.99 us (1%)
    unnamed x3, blocking collectives  360 us
    reduce_scatter x1, waiting for transfers between devices, on_device(): lax.psum_scatter(moments, 'comp', scatter_dimension=0, tiled=True)  114 us
    psum x1, blocking collectives, on_device(): lax.psum((owned_moments, owned_counts), 'grp')  35.3 us
    dot_general x4, matrix products, on_device(): jnp.dot(jnp.concatenate([squared, values], axis=1), all_coefficient.T, pr...  17.2 us
    all_to_all x1, starting transfers between devices, ends_save(): lax.all_to_all(jnp.stack([unit] * lax.axis_size(ax_name)), axis_name=ax_n...  15.2 us
  transfers between devices with their start and end apart: 4, of which 2 were waited for; matrix products, arithmetic and copies ran while one was open for 2% of the time, Pallas kernels for 0%

profile of v1, /device:TPU:1, one launch (start us, length us, event | category | flops | bytes accessed | tf_op | source)
XLA Modules:
  0.0 590.8 jit_solution(8780273197517670861)
XLA Ops:
  7.2 0.0 all-gather.3.cloned.1.call-start
  7.2 0.9 add_reduce_fusion.4
  8.1 0.6 pad_maximum_fusion
  8.7 0.0 all-gather.3.cloned.1.call-update
  8.7 0.0 reduce-scatter.2.cloned.1.call-start
  8.8 1.3 reduce_max.46
  10.1 1.9 exponential_reduce_fusion
  12.7 1.4 fusion.64
  14.7 1.3 subtract_subtract_fusion
  16.0 0.2 add_dynamic-update-slice_fusion
  16.2 112.2 %all-reduce = f32[1024]{0:T(1024)S(1)} all-reduce(f32[1024]{0:T(1024)S(1)} %add_dynamic-update-slice_fusion), channel_id=1, replica_groups=mesh['grp'=8,'comp'=64] {'comp'}, use_global_device_ids=true, to_apply=%add | all-reduce | flops 1024 | bytes 8192
  128.4 0.0 copy-start.3
  128.4 2.3 fusion.63
  130.8 0.0 copy-done.3
  130.8 1.4 fusion.38
  132.2 5.8 all-gather.3.cloned.1.call-done
  138.0 0.0 copy-start
  138.0 5.5 fusion.4
  143.5 0.0 copy-done
  143.5 0.0 copy-done.4
  143.5 3.6 fusion.12
  147.1 3.7 add_reduce_fusion
  150.8 4.4 fusion.3
  155.3 1.5 fusion.1
  156.8 0.0 copy-start.1
  156.8 0.0 copy-start.8
  156.8 0.0 copy-start.11
  156.9 1.4 divide_convert_fusion.2
  158.2 0.0 copy-done.8
  158.2 0.0 copy-done.11
  158.3 0.0 copy-start.6
  158.3 0.0 copy-start.10
  158.3 0.8 fusion.24
  159.0 0.2 copy-done.6
  159.2 0.1 copy-done.10
  159.3 0.7 fusion.20
  160.0 0.2 copy-done.5
  160.2 0.1 copy-done.9
  160.3 0.7 fusion.28
  161.1 0.0 copy-done.1
  161.1 0.2 copy-done.7
  161.3 2.1 add_add_fusion
  163.4 0.0 reduce-scatter.2.cloned.1.call-update
  164.0 0.0 copy-start.2
  164.1 0.2 fusion.49
  164.3 0.2 fusion.47
  164.6 0.3 fusion.45
  164.8 0.5 copy-done.2
  165.3 0.2 fusion.43
  165.5 104.4 %all-reduce.2 = f32[1024]{0:T(1024)S(1)} all-reduce(f32[1024]{0:T(1024)S(1)} %add_add_fusion.1), channel_id=3, replica_groups=mesh['grp'=8,'comp'=64] {'comp'}, use_global_device_ids=true, to_apply=%region_13.14.clone | all-reduce | flops 1024 | bytes 8192
  269.9 0.1 dynamic-slice.3
  270.0 114.3 %reduce-scatter.2.cloned.1.call-done = f32[16,512]{1,0:T(8,128)} async-done(((f32[1024,512]{1,0:T(8,128)}), f32[16,512]{1,0:T(8,128)}) %reduce-scatter.2.cloned.1.call-update) | async-done | bytes 32784 | tf_op jit(solution)/shard_map/reduce_scatter | solution.py:82
  384.2 35.3 %all-reduce.3 = (f32[16,512]{1,0:T(8,128)S(1)}, f32[16]{0:T(128)S(1)}) all-reduce(f32[16,512]{1,0:T(8,128)} %reduce-scatter.2.cloned.1.call-done, f32[16]{0:T(128)S(1)} %dynamic-slice.3), channel_id=1, replica_groups=mesh['grp'=8,'comp'=64] {'grp'}, use_global_device_ids=true, to_apply=%region_12.13 | all-reduce | flops 8208 | bytes 65664 | tf_op jit(solution)/shard_map/psum | solution.py:85
  419.6 0.1 log_dynamic-update-slice_fusion
  419.7 0.7 fusion.41
  420.4 1.1 stack.2
  421.5 15.2 %all-to-all-start = ((f32[64,16,256]{2,1,0:T(8,128)}), f32[64,16,256]{2,1,0:T(8,128)S(1)}, u32[]{:S(2)}, u32[]{:S(2)}) async-start(f32[64,16,256]{2,1,0:T(8,128)} %stack.2), calls=%async_computation.1 | async-start | bytes 2097152 | tf_op jit(solution)/shard_map/all_to_all | solution.py:10
  436.7 0.0 all-gather.5.cloned.1.call-start
  436.7 0.7 all-gather.5.cloned.1.call-update
  437.4 0.6 pad_maximum_fusion.1
  438.0 143.0 %all-reduce.1 = f32[1024]{0:T(1024)} all-reduce(f32[1024]{0:T(1024)S(1)} %get-tuple-element.41), channel_id=1, replica_groups=mesh['grp'=8,'comp'=64] {'comp'}, use_global_device_ids=true, to_apply=%add.1 | all-reduce | flops 1024 | bytes 8192
  581.0 0.0 all-to-all-done
  581.0 2.3 copy.12
  583.3 1.0 copy.13
  (10 shorter events, 0.0 us)
Async XLA Ops:
  7.2 130.9 %all-gather.3.cloned.1.call-start = ((), (), s32[]{:S(2)}) async-start(), calls=%async_computation.2 | async-start | bytes 2129920 | tf_op jit(solution)/shard_map/all_gather | solution.py:45
  8.7 375.5 %reduce-scatter.2.cloned.1.call-start = ((), (), s32[]{:S(2)}) async-start(), calls=%async_computation.3 | async-start | bytes 2129920 | tf_op jit(solution)/shard_map/reduce_scatter | solution.py:82
  128.4 2.3 copy-start.3
  138.0 5.5 copy-start
  138.0 5.5 copy-start.4
  156.8 4.2 copy-start.1
  156.8 1.4 copy-start.8
  156.8 1.4 copy-start.11
  158.3 1.0 copy-start.6
  158.3 1.0 copy-start.10
  159.3 0.9 copy-start.5
  159.3 1.0 copy-start.9
  160.3 0.9 copy-start.7
  164.0 1.2 copy-start.2
  421.5 159.6 %all-to-all-start = ((f32[64,16,256]{2,1,0:T(8,128)}), f32[64,16,256]{2,1,0:T(8,128)S(1)}, u32[]{:S(2)}, u32[]{:S(2)}) async-start(f32[64,16,256]{2,1,0:T(8,128)} %stack.2), calls=%async_computation.1 | async-start | bytes 2097152 | tf_op jit(solution)/shard_map/all_to_all | solution.py:10
  436.7 144.4 %all-gather.5.cloned.1.call-start = ((), (), s32[]{:S(2)}) async-start(), calls=%async_computation.4 | async-start | bytes 1064960 | tf_op jit(solution)/shard_map/all_gather | solution.py:90
Sparse Core Ops, SparseCore 0:
  10.2 127.8 all-gather.2
  163.5 220.6 reduce-scatter.1
  440.4 124.1 all-gather.4
